TPU v7x, 32 devices: a whole 2x2x4 slice. The times are simulated.
32 devices in a mesh: ctx: 4 (over z), head: 4 (over y, x), seg: 2 (over core).
Axes of the slice: x: 2, y: 2, z: 4, core: 2. Of those that a mesh axis runs over, the one named last changes fastest.
Arguments:
- tokens_x: bfloat16 [4096, 2560], P(('ctx', 'seg'), 'head'), may hold values from -6 to 6
- gate_weight: bfloat16 [64, 3, 2560], P(None, None, 'head'), may hold values from -0.15625 to 0.15625
- queries: bfloat16 [4096, 64, 192], P(('ctx', 'seg'), 'head'), may hold values from -48 to 48
- keys: bfloat16 [4096, 4, 192], P(('ctx', 'seg'), 'head'), may hold values from -7 to 7
- values: bfloat16 [4096, 4, 128], P(('ctx', 'seg'), 'head'), may hold values from -24 to 24
- comp_key_weight: bfloat16 [4, 32, 192], P('head'), may hold values from -1 to 1
- comp_value_weight: bfloat16 [4, 32, 128], P('head'), may hold values from -1 to 1
- selected: int32 [32, 4, 16], P(('ctx', 'seg'), 'head'), may hold values from -1 to 63, as said below
Outputs:
- attention: bfloat16 [4096, 64, 128], P(('ctx', 'seg'), 'head')
Inputs may be any that keep to these rules, and one draw needn't show every extreme that they name: Each list names the tile's own fine blocks and block 0, then further blocks; live entries are distinct and at most the tile's last fine block; -1 marks an empty entry. For the tiles of one device (one block of 512 tokens) and one group, the blocks selected from the segment of 512 tokens of any other device number at most 1, and some device reaches it.
All inputs are finite; a program needn't handle non-finite values.
Results may differ from a plain program's by a relative error of at most 0.0059.
Values may be sent and summed in bfloat16 or wider, within the bound.
A program may use at most 128 MiB of HBM per device.

v0:
```python
import jax
import jax.numpy as jnp
from jax import lax
from jax.sharding import PartitionSpec as P

TILE = 128
BLK_S = 64
BLK_C = 32
NSEL = 16
WINDOW = 512


def shifted(value, axis, steps):
    count = lax.axis_size(axis)
    leading, last = (max(0, -steps), min(count, count - steps))
    return lax.ppermute(value, axis, [(source, source + steps) for source in range(leading, last)])


def attend(query, keys_part, values_part, allowed):
    scores = jnp.einsum(
        "rhd,kd->hrk", query, keys_part, preferred_element_type=jnp.float32
    ) * keys_part.shape[-1] ** (-0.5)
    scores = jnp.where(allowed[None], scores, -1e30)
    highest = jnp.max(scores, axis=-1, keepdims=True)
    weights = jnp.where(allowed[None], jnp.exp(scores - highest), 0.0)
    total = jnp.sum(weights, axis=-1)
    rounded = weights.astype(jnp.bfloat16)
    summed = jnp.einsum("hrk,kv->rhv", rounded, values_part, preferred_element_type=jnp.float32)
    return summed / jnp.maximum(total, 1.0).T[:, :, None]


def on_device(
    tokens_x, gate_weight, queries, keys, values, comp_key_weight, comp_value_weight, selected
):
    local_count = queries.shape[0]
    head_count = queries.shape[1]
    key_width = keys.shape[2]
    place = lax.axis_index(("ctx", "seg"))
    offset = place * local_count
    rows = gate_weight
    gates = jax.nn.sigmoid(
        lax.psum_scatter(
            jnp.einsum("hcd,td->hct", rows, tokens_x, preferred_element_type=jnp.float32),
            "head",
            scatter_dimension=0,
            tiled=True,
        )
    )
    own_keys = keys[:, 0]
    own_values = values[:, 0]
    packed = jnp.concatenate([own_keys, own_values], axis=1)
    coarse_local = local_count // BLK_C
    squeezed_keys = jnp.sum(
        own_keys.astype(jnp.float32).reshape(coarse_local, BLK_C, key_width)
        * comp_key_weight[0].astype(jnp.float32)[None],
        axis=1,
    )
    squeezed_values = jnp.sum(
        own_values.astype(jnp.float32).reshape(coarse_local, BLK_C, -1)
        * comp_value_weight[0].astype(jnp.float32)[None],
        axis=1,
    )
    coarse_packed = jnp.concatenate(
        [squeezed_keys.astype(jnp.bfloat16), squeezed_values.astype(jnp.bfloat16)], axis=1
    )
    coarse = lax.all_gather(coarse_packed, ("ctx", "seg"), axis=0, tiled=True)
    coarse_end = jnp.arange(coarse.shape[0], dtype=jnp.int32) * BLK_C + BLK_C - 1
    previous = shifted(packed, ("ctx", "seg"), 1)
    extended = jnp.concatenate([previous, packed], axis=0)
    chosen_all = selected[:, 0, :]
    blocks_all = jnp.maximum(chosen_all, 0)
    everything = lax.all_gather(packed, ("ctx", "seg"), axis=0, tiled=True)
    picked = everything.reshape(-1, BLK_S, packed.shape[1])[blocks_all]

    def one_tile(tile):
        begin = tile * TILE
        rows = offset + begin + jnp.arange(TILE, dtype=jnp.int32)
        query = lax.dynamic_slice_in_dim(queries, begin, TILE, 0)
        gate = lax.dynamic_slice_in_dim(gates, begin, TILE, 2)
        near = lax.dynamic_slice_in_dim(extended, begin + local_count - WINDOW, WINDOW + TILE, 0)
        near_pos = offset + begin - WINDOW + jnp.arange(WINDOW + TILE, dtype=jnp.int32)
        near_ok = (
            (near_pos[None, :] >= 0)
            & (near_pos[None, :] <= rows[:, None])
            & (near_pos[None, :] > rows[:, None] - WINDOW)
        )
        coarse_ok = coarse_end[None, :] <= rows[:, None]
        chosen = chosen_all[tile]
        blocks = jnp.maximum(chosen, 0)
        fine = picked[tile].reshape(NSEL * BLK_S, packed.shape[1])
        fine_pos = (blocks[:, None] * BLK_S + jnp.arange(BLK_S, dtype=jnp.int32)[None, :]).reshape(
            -1
        )
        live = jnp.repeat(chosen >= 0, BLK_S)
        fine_ok = live[None, :] & (fine_pos[None, :] <= rows[:, None])
        coarse_out = attend(query, coarse[:, :key_width], coarse[:, key_width:], coarse_ok)
        fine_out = attend(query, fine[:, :key_width], fine[:, key_width:], fine_ok)
        window_out = attend(query, near[:, :key_width], near[:, key_width:], near_ok)
        mixed = gate[:, 0, :].T[:, :, None] * coarse_out + gate[:, 1, :].T[:, :, None] * fine_out
        mixed = mixed + gate[:, 2, :].T[:, :, None] * window_out
        return mixed.astype(jnp.bfloat16)

    tiles = lax.map(one_tile, jnp.arange(local_count // TILE, dtype=jnp.int32))
    return tiles.reshape(local_count, head_count, -1)


def solution(mesh):
    in_specs = (
        P(("ctx", "seg"), "head"),
        P(None, None, "head"),
        P(("ctx", "seg"), "head", None),
        P(("ctx", "seg"), "head", None),
        P(("ctx", "seg"), "head", None),
        P("head", None, None),
        P("head", None, None),
        P(("ctx", "seg"), "head", None),
    )
    out_specs = P(("ctx", "seg"), "head", None)
    return jax.shard_map(
        on_device, mesh=mesh, in_specs=in_specs, out_specs=out_specs, check_vma=False
    )
```

profile of v0, /device:TPU:0, one launch (start us, length us, event | category | flops | bytes accessed | tf_op | source)
XLA Modules:
  0.0 226.0 jit_solution(13113540799511272979)
XLA Ops:
  16.2 15.6 %all_gather.6 = bf16[128,320]{1,0:T(8,128)(2,1)S(1)} all-gather(bf16[16,320]{1,0:T(8,128)(2,1)S(1)} %pad_maximum_fusion.1), channel_id=1, replica_groups=mesh['ctx'=4,'head'=4,'seg'=2] {'ctx','seg'}, dimensions={0}, use_global_device_ids=true | all-gather | bytes 92160 | tf_op jit(solution)/shard_map/all_gather | solution.py:66
  32.5 5.9 %reduce-scatter.2.cloned.1.call-done = f32[16,3,512]{2,0,1:T(8,128)} async-done(((f32[64,3,512]{2,0,1:T(8,128)}), f32[16,3,512]{2,0,1:T(8,128)}) %reduce-scatter.2.cloned.1.call-update) | async-done | bytes 98320 | tf_op jit(solution)/shard_map/reduce_scatter | solution.py:42
  39.4 15.5 %all-gather.2.cloned.1.call-done = bf16[4096,320]{1,0:T(8,128)(2,1)} async-done(((bf16[512,320]{1,0:T(8,128)(2,1)}), bf16[4096,320]{1,0:T(8,128)(2,1)}) %all-gather.2.cloned.1.call-update) | async-done | bytes 2621456 | tf_op jit(solution)/shard_map/all_gather | solution.py:72
  54.9 4.5 %gather_fusion = bf16[64,64,320]{2,1,0:T(8,128)(2,1)} fusion(bf16[64,64,320]{2,1,0:T(8,128)(2,1)} %bitcast.193, s32[1024]{0:T(1024)S(1)} %pad_clamp_fusion), kind=kCustom, calls=%fused_computation | custom fusion | bytes 5243136 | tf_op jit(solution)/shard_map/gather | solution.py:73
  59.4 159.2 %while.16 = (s32[]{:T(128)}, bf16[4,128,16,128]{3,2,1,0:T(8,128)(2,1)}, s32[4]{0:T(128)S(1)}, f32[16,3,512]{2,0,1:T(8,128)S(1)}, s32[]{:T(128)}, /*index=5*/bf16...) while((s32[]{:T(128)}, ...), condition=%wide.region_10.11_spmd.clone, body=%wide.region_3.10_spmd.clone.sunk | while | flops 2376428544 | bytes 36854732 | solution.py:103
  60.8 4.3 %fusion.126 = f32[640,128,16]{1,0,2:T(8,128)} fusion(bf16[512,16,192]{0,2,1:T(8,128)(2,1)} %get-tuple-element.459, s32[]{:T(128)S(6)} %select_n.150, bf16[1024,320]{0,1:T(8,128)(2,1)S(1)} %get-tuple-element.463, s32[]{:T(128)S(6)} %select_n.151), kind=kOutput, calls=%fused_computation.46.clone.1 | convolution fusion | flops 503316480 | bytes 6275080 | tf_op jit(solution)/shard_map/while/body/eval_jaxpr/rhd,kd->hrk/dot_general | solution.py:20
  65.4 8.3 %fusion.127 = (f32[16,128]{1,0:T(8,128)S(1)}, bf16[16,128,640]{1,2,0:T(8,128)(2,1)}) fusion(f32[640,128,16]{1,0,2:T(8,128)} %fusion.126, pred[128,640]{0,1:T(8,128)(4,1)S(1)} %compare_and_fusion.4), kind=kOutput, calls=%fused_computation.103.clone.1 | output fusion | flops 10486399 | bytes 7954432 | tf_op jit(solution)/shard_map/while/body/eval_jaxpr/sub | solution.py:25
  81.7 6.9 %fusion.129 = (f32[16,128]{1,0:T(8,128)S(1)}, bf16[16,128,1024]{1,2,0:T(8,128)(2,1)}) fusion(pred[128,1024]{0,1:T(8,128)(4,1)S(1)} %compare_and_fusion.5, bf16[512,16,192]{0,2,1:T(8,128)(2,1)} %get-tuple-element.459, s32[]{:T(128)S(6)} %select_n.150, bf16[1024,320]{1,0:T(8,128)(2,1)S(1)} %bitcast.187), kind=kOutput, calls=%fused_computation.104.clone.1 | convolution fusion | flops 817890304 | bytes 5775364 | tf_op jit(solution)/shard_map/while/body/eval_jaxpr/sub | solution.py:25
  88.5 5.4 %fusion.130 = f32[128,16,128]{2,0,1:T(8,128)} fusion(bf16[16,128,1024]{1,2,0:T(8,128)(2,1)} %get-tuple-element.408, f32[128,16]{0,1:T(8,128)S(1)} %maximum_bitcast_fusion.7, f32[128,16]{0,1:T(8,128)S(1)} %get-tuple-element.410, bf16[1024,320]{1,0:T(8,128)(2,1)S(1)} %bitcast.188), kind=kOutput, calls=%fused_computation.37.clone.1 | convolution fusion | flops 537395200 | bytes 5521408 | tf_op jit(solution)/shard_map/while/body/eval_jaxpr/hrk,kv->rhv/dot_general | solution.py:28
  100.5 4.3 %fusion.126 = f32[640,128,16]{1,0,2:T(8,128)} fusion(bf16[512,16,192]{0,2,1:T(8,128)(2,1)} %get-tuple-element.459, s32[]{:T(128)S(6)} %select_n.150, bf16[1024,320]{0,1:T(8,128)(2,1)S(1)} %get-tuple-element.463, s32[]{:T(128)S(6)} %select_n.151), kind=kOutput, calls=%fused_computation.46.clone.1 | convolution fusion | flops 503316480 | bytes 6275080 | tf_op jit(solution)/shard_map/while/body/eval_jaxpr/rhd,kd->hrk/dot_general | solution.py:20
  105.1 8.3 %fusion.127 = (f32[16,128]{1,0:T(8,128)S(1)}, bf16[16,128,640]{1,2,0:T(8,128)(2,1)}) fusion(f32[640,128,16]{1,0,2:T(8,128)} %fusion.126, pred[128,640]{0,1:T(8,128)(4,1)S(1)} %compare_and_fusion.4), kind=kOutput, calls=%fused_computation.103.clone.1 | output fusion | flops 10486399 | bytes 7954432 | tf_op jit(solution)/shard_map/while/body/eval_jaxpr/sub | solution.py:25
  113.5 4.0 %fusion.128 = f32[128,16,128]{2,0,1:T(8,128)} fusion(bf16[16,128,640]{1,2,0:T(8,128)(2,1)} %get-tuple-element.405, f32[128,16]{0,1:T(8,128)S(1)} %maximum_bitcast_fusion.6, f32[128,16]{0,1:T(8,128)S(1)} %get-tuple-element.407, bf16[1024,320]{0,1:T(8,128)(2,1)S(1)} %get-tuple-element.463, s32[]{:T(128)S(6)} %select_n.151, s32[]{:T(128)S(6)} %add.284), kind=kOutput, calls=%fused_computation.36.clone.1 | convolution fusion | flops 336068608 | bytes 3850248 | tf_op jit(solution)/shard_map/while/body/eval_jaxpr/hrk,kv->rhv/dot_general | solution.py:28
  121.4 6.9 %fusion.129 = (f32[16,128]{1,0:T(8,128)S(1)}, bf16[16,128,1024]{1,2,0:T(8,128)(2,1)}) fusion(pred[128,1024]{0,1:T(8,128)(4,1)S(1)} %compare_and_fusion.5, bf16[512,16,192]{0,2,1:T(8,128)(2,1)} %get-tuple-element.459, s32[]{:T(128)S(6)} %select_n.150, bf16[1024,320]{1,0:T(8,128)(2,1)S(1)} %bitcast.187), kind=kOutput, calls=%fused_computation.104.clone.1 | convolution fusion | flops 817890304 | bytes 5775364 | tf_op jit(solution)/shard_map/while/body/eval_jaxpr/sub | solution.py:25
  128.3 5.4 %fusion.130 = f32[128,16,128]{2,0,1:T(8,128)} fusion(bf16[16,128,1024]{1,2,0:T(8,128)(2,1)} %get-tuple-element.408, f32[128,16]{0,1:T(8,128)S(1)} %maximum_bitcast_fusion.7, f32[128,16]{0,1:T(8,128)S(1)} %get-tuple-element.410, bf16[1024,320]{1,0:T(8,128)(2,1)S(1)} %bitcast.188), kind=kOutput, calls=%fused_computation.37.clone.1 | convolution fusion | flops 537395200 | bytes 5521408 | tf_op jit(solution)/shard_map/while/body/eval_jaxpr/hrk,kv->rhv/dot_general | solution.py:28
  140.3 4.3 %fusion.126 = f32[640,128,16]{1,0,2:T(8,128)} fusion(bf16[512,16,192]{0,2,1:T(8,128)(2,1)} %get-tuple-element.459, s32[]{:T(128)S(6)} %select_n.150, bf16[1024,320]{0,1:T(8,128)(2,1)S(1)} %get-tuple-element.463, s32[]{:T(128)S(6)} %select_n.151), kind=kOutput, calls=%fused_computation.46.clone.1 | convolution fusion | flops 503316480 | bytes 6275080 | tf_op jit(solution)/shard_map/while/body/eval_jaxpr/rhd,kd->hrk/dot_general | solution.py:20
  144.9 8.3 %fusion.127 = (f32[16,128]{1,0:T(8,128)S(1)}, bf16[16,128,640]{1,2,0:T(8,128)(2,1)}) fusion(f32[640,128,16]{1,0,2:T(8,128)} %fusion.126, pred[128,640]{0,1:T(8,128)(4,1)S(1)} %compare_and_fusion.4), kind=kOutput, calls=%fused_computation.103.clone.1 | output fusion | flops 10486399 | bytes 7954432 | tf_op jit(solution)/shard_map/while/body/eval_jaxpr/sub | solution.py:25
  153.3 4.0 %fusion.128 = f32[128,16,128]{2,0,1:T(8,128)} fusion(bf16[16,128,640]{1,2,0:T(8,128)(2,1)} %get-tuple-element.405, f32[128,16]{0,1:T(8,128)S(1)} %maximum_bitcast_fusion.6, f32[128,16]{0,1:T(8,128)S(1)} %get-tuple-element.407, bf16[1024,320]{0,1:T(8,128)(2,1)S(1)} %get-tuple-element.463, s32[]{:T(128)S(6)} %select_n.151, s32[]{:T(128)S(6)} %add.284), kind=kOutput, calls=%fused_computation.36.clone.1 | convolution fusion | flops 336068608 | bytes 3850248 | tf_op jit(solution)/shard_map/while/body/eval_jaxpr/hrk,kv->rhv/dot_general | solution.py:28
  161.3 6.9 %fusion.129 = (f32[16,128]{1,0:T(8,128)S(1)}, bf16[16,128,1024]{1,2,0:T(8,128)(2,1)}) fusion(pred[128,1024]{0,1:T(8,128)(4,1)S(1)} %compare_and_fusion.5, bf16[512,16,192]{0,2,1:T(8,128)(2,1)} %get-tuple-element.459, s32[]{:T(128)S(6)} %select_n.150, bf16[1024,320]{1,0:T(8,128)(2,1)S(1)} %bitcast.187), kind=kOutput, calls=%fused_computation.104.clone.1 | convolution fusion | flops 817890304 | bytes 5775364 | tf_op jit(solution)/shard_map/while/body/eval_jaxpr/sub | solution.py:25
  168.1 5.4 %fusion.130 = f32[128,16,128]{2,0,1:T(8,128)} fusion(bf16[16,128,1024]{1,2,0:T(8,128)(2,1)} %get-tuple-element.408, f32[128,16]{0,1:T(8,128)S(1)} %maximum_bitcast_fusion.7, f32[128,16]{0,1:T(8,128)S(1)} %get-tuple-element.410, bf16[1024,320]{1,0:T(8,128)(2,1)S(1)} %bitcast.188), kind=kOutput, calls=%fused_computation.37.clone.1 | convolution fusion | flops 537395200 | bytes 5521408 | tf_op jit(solution)/shard_map/while/body/eval_jaxpr/hrk,kv->rhv/dot_general | solution.py:28
  180.1 4.3 %fusion.126 = f32[640,128,16]{1,0,2:T(8,128)} fusion(bf16[512,16,192]{0,2,1:T(8,128)(2,1)} %get-tuple-element.459, s32[]{:T(128)S(6)} %select_n.150, bf16[1024,320]{0,1:T(8,128)(2,1)S(1)} %get-tuple-element.463, s32[]{:T(128)S(6)} %select_n.151), kind=kOutput, calls=%fused_computation.46.clone.1 | convolution fusion | flops 503316480 | bytes 6275080 | tf_op jit(solution)/shard_map/while/body/eval_jaxpr/rhd,kd->hrk/dot_general | solution.py:20
  184.8 8.3 %fusion.127 = (f32[16,128]{1,0:T(8,128)S(1)}, bf16[16,128,640]{1,2,0:T(8,128)(2,1)}) fusion(f32[640,128,16]{1,0,2:T(8,128)} %fusion.126, pred[128,640]{0,1:T(8,128)(4,1)S(1)} %compare_and_fusion.4), kind=kOutput, calls=%fused_computation.103.clone.1 | output fusion | flops 10486399 | bytes 7954432 | tf_op jit(solution)/shard_map/while/body/eval_jaxpr/sub | solution.py:25
  193.1 4.0 %fusion.128 = f32[128,16,128]{2,0,1:T(8,128)} fusion(bf16[16,128,640]{1,2,0:T(8,128)(2,1)} %get-tuple-element.405, f32[128,16]{0,1:T(8,128)S(1)} %maximum_bitcast_fusion.6, f32[128,16]{0,1:T(8,128)S(1)} %get-tuple-element.407, bf16[1024,320]{0,1:T(8,128)(2,1)S(1)} %get-tuple-element.463, s32[]{:T(128)S(6)} %select_n.151, s32[]{:T(128)S(6)} %add.284), kind=kOutput, calls=%fused_computation.36.clone.1 | convolution fusion | flops 336068608 | bytes 3850248 | tf_op jit(solution)/shard_map/while/body/eval_jaxpr/hrk,kv->rhv/dot_general | solution.py:28
  201.1 6.9 %fusion.129 = (f32[16,128]{1,0:T(8,128)S(1)}, bf16[16,128,1024]{1,2,0:T(8,128)(2,1)}) fusion(pred[128,1024]{0,1:T(8,128)(4,1)S(1)} %compare_and_fusion.5, bf16[512,16,192]{0,2,1:T(8,128)(2,1)} %get-tuple-element.459, s32[]{:T(128)S(6)} %select_n.150, bf16[1024,320]{1,0:T(8,128)(2,1)S(1)} %bitcast.187), kind=kOutput, calls=%fused_computation.104.clone.1 | convolution fusion | flops 817890304 | bytes 5775364 | tf_op jit(solution)/shard_map/while/body/eval_jaxpr/sub | solution.py:25
  207.9 5.4 %fusion.130 = f32[128,16,128]{2,0,1:T(8,128)} fusion(bf16[16,128,1024]{1,2,0:T(8,128)(2,1)} %get-tuple-element.408, f32[128,16]{0,1:T(8,128)S(1)} %maximum_bitcast_fusion.7, f32[128,16]{0,1:T(8,128)S(1)} %get-tuple-element.410, bf16[1024,320]{1,0:T(8,128)(2,1)S(1)} %bitcast.188), kind=kOutput, calls=%fused_computation.37.clone.1 | convolution fusion | flops 537395200 | bytes 5521408 | tf_op jit(solution)/shard_map/while/body/eval_jaxpr/hrk,kv->rhv/dot_general | solution.py:28
  (126 shorter events, 46.5 us)
Async XLA Ops:
  7.4 1.1 copy-start
  7.4 8.6 %copy-start.1 = (bf16[512,1,128]{2,0,1:T(8,128)(2,1)S(1)}, bf16[512,1,128]{2,0,1:T(8,128)(2,1)}, u32[]{:S(2)}) copy-start(bf16[512,1,128]{2,0,1:T(8,128)(2,1)} %param.14) | copy-start | bytes 393220
  7.4 8.6 %copy-start.3 = (bf16[1,32,128]{2,1,0:T(8,128)(2,1)S(1)}, bf16[1,32,128]{2,1,0:T(8,128)(2,1)}, u32[]{:S(2)}) copy-start(bf16[1,32,128]{2,1,0:T(8,128)(2,1)} %param.16) | copy-start | bytes 24580
  7.4 8.7 %copy-start.2 = (bf16[1,32,192]{2,1,0:T(8,128)(2,1)S(1)}, bf16[1,32,192]{2,1,0:T(8,128)(2,1)}, u32[]{:S(2)}) copy-start(bf16[1,32,192]{2,1,0:T(8,128)(2,1)} %param.15) | copy-start | bytes 36868
  7.4 24.6 %copy-start.4 = (s32[4,1,16]{2,1,0:T(1,128)S(1)}, s32[4,1,16]{2,1,0:T(1,128)}, u32[]{:S(2)}) copy-start(s32[4,1,16]{2,1,0:T(1,128)} %param.17) | copy-start | bytes 772
  7.4 31.1 %reduce-scatter.2.cloned.1.call-start = ((), (), s32[]{:S(2)}) async-start(), calls=%async_computation.1 | async-start | bytes 491520 | tf_op jit(solution)/shard_map/reduce_scatter | solution.py:42
  10.6 44.3 %all-gather.2.cloned.1.call-start = ((), (), s32[]{:S(2)}) async-start(), calls=%async_computation.2 | async-start | bytes 3538944 | tf_op jit(solution)/shard_map/all_gather | solution.py:72
  13.5 18.6 %collective-permute-start = (bf16[512,320]{1,0:T(8,128)(2,1)}, bf16[512,320]{1,0:T(8,128)(2,1)S(1)}, u32[]{:S(2)}, u32[]{:S(2)}) collective-permute-start(bf16[512,320]{1,0:T(8,128)(2,1)} %pad_maximum_fusion), channel_id=1, source_target_pairs={{0,1},{1,8},{8,9},{9,16},{16,17},{17,24},{24,25},{2,3},{3,10},{10,... | collective-permute-start | bytes 983048 | tf_op jit(solution)/shard_map/ppermute | solution.py:16
Sparse Core Ops, SparseCore 0:
  11.0 27.4 reduce-scatter.1
Sparse Core Ops, SparseCore 1:
  13.6 41.2 all-gather.1
where the time goes:
time: 228 us; the launch traced here: 226 us
  matrix products  100 us (44%)
  other arithmetic  39.5 us (17%)
  waiting for transfers between devices  21.5 us (9%)
  local copies, waits for them, and re-layouts  20.6 us (9%)
  blocking collectives  15.6 us (7%)
  between operations  15 us (7%)
  loops' own time  11.2 us (5%)
  starting transfers between devices  2.5 us (1%)
    dot_general x12, matrix products, attend(): jnp.einsum('hrk,kv->rhv', rounded, values_part, preferred_element_type=jn...  46.3 us
    sub x8, matrix products, attend(): weights = jnp.where(allowed[None], jnp.exp(scores - highest), 0.0)  34.5 us
    sub x4, other arithmetic, attend(): weights = jnp.where(allowed[None], jnp.exp(scores - highest), 0.0)  33.2 us
    dot_general x4, matrix products, attend(): jnp.einsum('rhd,kd->hrk', query, keys_part, preferred_element_type=jnp.fl...  17.4 us
    all_gather x1, blocking collectives, on_device(): coarse = lax.all_gather(coarse_packed, ('ctx', 'seg'), axis=0, tiled=True)  15.6 us
    all_gather x1, waiting for transfers between devices, on_device(): everything = lax.all_gather(packed, ('ctx', 'seg'), axis=0, tiled=True)  15.5 us
    another operation x1, loops' own time, on_device(): tiles = lax.map(one_tile, jnp.arange(local_count // TILE, dtype=jnp.int32))  11.2 us
    reduce_scatter x1, waiting for transfers between devices, on_device(): lax.psum_scatter(jnp.einsum('hcd,td->hct', rows, tokens_x, preferred_elem...  5.93 us
  transfers between devices with their start and end apart: 3, of which 2 were waited for; matrix products, arithmetic and copies ran while one was open for 2% of the time, Pallas kernels for 0%

commit v1 on v0

v1 whole, which is shorter than its diff:
```python
import functools

import jax
import jax.numpy as jnp
from jax import lax
from jax.experimental import pallas as pl
from jax.experimental.pallas import tpu as pltpu
from jax.sharding import PartitionSpec as P

TILE = 128
BLK_S = 64
BLK_C = 32
NSEL = 16
WINDOW = 512
HEADS = 4
BOUND = 40.0

MESH = pl.DeviceIdType.MESH
NT = (((1,), (1,)), ((), ()))
NN = (((1,), (0,)), ((), ()))


def dot(a, b, dims=NN):
    return lax.dot_general(a, b, dims, preferred_element_type=jnp.float32)


def exchange_kernel(
    n, segs, heads,
    x_ref, w_ref, kt_ref, v_ref, cwk_ref, cwv_ref, sel_ref,
    g_ref, pk_ref, pv_ref, ck_ref, cv_ref, bk_ref, bv_ref,
    part, got, cks, cvs, sels, stk, stv, ssem, rsem, gs, gr,
):
    local = v_ref.shape[0]
    coarse = local // BLK_C
    share = g_ref.shape[0]
    ctx, seg, head = lax.axis_index("ctx"), lax.axis_index("seg"), lax.axis_index("head")
    me = ctx * segs + seg

    def ring(steps):
        other = lax.rem(me + steps + n, n)
        return {"ctx": other // segs, "seg": lax.rem(other, segs)}

    def peer(steps):
        return {"head": lax.rem(head + steps + heads, heads)}

    barrier = pltpu.get_barrier_semaphore()
    for r in range(1, n):
        pl.semaphore_signal(barrier, inc=1, device_id=ring(r), device_id_type=MESH)
    for r in range(1, heads):
        pl.semaphore_signal(barrier, inc=1, device_id=peer(r), device_id_type=MESH)

    cks[...] = jnp.sum(
        kt_ref[...].astype(jnp.float32).T.reshape(coarse, BLK_C, -1)
        * cwk_ref[...].astype(jnp.float32)[None], axis=1
    ).astype(jnp.bfloat16)
    cvs[...] = jnp.sum(
        v_ref[...].astype(jnp.float32).reshape(coarse, BLK_C, -1)
        * cwv_ref[...].astype(jnp.float32)[None], axis=1
    ).astype(jnp.bfloat16)

    pl.semaphore_wait(barrier, n - 1 + heads - 1)

    def send(src, dst, kind, slot, where):
        copy = pltpu.make_async_remote_copy(
            src_ref=src, dst_ref=dst, send_sem=ssem.at[kind, slot],
            recv_sem=rsem.at[kind, slot], device_id=where, device_id_type=MESH,
        )
        copy.start()
        return copy

    lists = [send(sel_ref, sels.at[r - 1], 0, r - 1, ring(-r)) for r in range(1, n)]
    rest = [send(kt_ref, pk_ref, 5, 0, ring(1)), send(v_ref, pv_ref, 5, 1, ring(1))]

    gates = dot(w_ref[...], x_ref[...], NT)
    hc = share // 3
    for h in range(heads):
        for c in range(3):
            first = (c * heads + h) * hc
            part[h, c * hc:(c + 1) * hc] = gates[first:first + hc]

    mine = pl.ds(pl.multiple_of(me * coarse, coarse), coarse)
    for r in range(1, n):
        rest.append(send(cks, ck_ref.at[mine], 1, r - 1, ring(r)))
        rest.append(send(cvs, cv_ref.at[mine], 2, r - 1, ring(r)))
    ck_ref[mine, :] = cks[...]
    cv_ref[mine, :] = cvs[...]
    sums = []
    for r in range(1, heads):
        copy = pltpu.make_async_remote_copy(
            src_ref=part.at[lax.rem(head + r, heads)], dst_ref=got.at[r - 1],
            send_sem=gs.at[r - 1], recv_sem=gr.at[r - 1],
            device_id=peer(r), device_id_type=MESH,
        )
        copy.start()
        sums.append(copy)

    per = local // BLK_S
    for r in range(1, n):
        lists[r - 1].wait()
        asked = sels[r - 1]
        hit = (asked >= me * per) & (asked < (me + 1) * per)
        want = jnp.where(hit, asked - me * per, 0)
        want = jnp.max(jnp.max(want, axis=1, keepdims=True), axis=0, keepdims=True)
        ahead = lax.broadcasted_iota(jnp.int32, (BLK_S, local), 1) - lax.broadcasted_iota(
            jnp.int32, (BLK_S, local), 0
        )
        pick = jnp.where(ahead == want * BLK_S, 1.0, 0.0).astype(jnp.bfloat16)
        stk[r - 1] = dot(pick, kt_ref[...], NT).astype(jnp.bfloat16)
        stv[r - 1] = dot(pick, v_ref[...]).astype(jnp.bfloat16)
    bk_ref[(n - 1) * BLK_S:, :] = jnp.zeros((BLK_S, bk_ref.shape[1]), jnp.bfloat16)
    bv_ref[(n - 1) * BLK_S:, :] = jnp.zeros((BLK_S, bv_ref.shape[1]), jnp.bfloat16)
    for r in range(1, n):
        rows = pl.ds((r - 1) * BLK_S, BLK_S)
        rest.append(send(stk.at[r - 1], bk_ref.at[rows], 3, r - 1, ring(r)))
        rest.append(send(stv.at[r - 1], bv_ref.at[rows], 4, r - 1, ring(r)))

    for copy in sums:
        copy.wait()
    total = part[head]
    for r in range(1, heads):
        total = total + got[r - 1]
    g_ref[...] = jax.nn.sigmoid(total)
    for copy in rest:
        copy.wait()


def attention_kernel(
    n, segs, hc, local,
    sel_ref, q_ref, kt_ref, v_ref, pk_ref, pv_ref, bk_ref, bv_ref, ck_ref, cv_ref, g_ref,
    o_ref,
    kw, vtw, vtp, lw, lp, lc, mixed_ref, knorm,
):
    f32, bf16 = jnp.float32, jnp.bfloat16
    me = lax.axis_index("ctx") * segs + lax.axis_index("seg")
    tile = pl.program_id(0)
    sub = pl.program_id(1)
    rows = TILE * HEADS
    span = WINDOW + TILE
    dk = kt_ref.shape[0]
    dv = v_ref.shape[1]
    nc = ck_ref.shape[0]
    npk = (n - 1) * BLK_S
    per = local // BLK_S
    coef = dk ** -0.5

    @pl.when((tile == 0) & (sub == 0))
    def _():
        kw[:WINDOW] = pk_ref[:, local - WINDOW:].astype(f32).T.astype(bf16)
        kw[WINDOW:] = kt_ref[...].astype(f32).T.astype(bf16)
        vtw[:, :WINDOW] = pv_ref[local - WINDOW:, :].astype(f32).T.astype(bf16)
        vtw[:, WINDOW:] = v_ref[...].astype(f32).T.astype(bf16)
        vtp[...] = bv_ref[...].astype(f32).T.astype(bf16)
        lc[:dv] = cv_ref[...].astype(f32).T.astype(bf16)
        lc[dv:] = jnp.where(
            lax.broadcasted_iota(jnp.int32, (16, nc), 0) == 0, 1.0, 0.0
        ).astype(bf16)
        top = jnp.zeros((1, 1), f32)
        for ref in (kw, bk_ref, ck_ref):
            part = ref[...].astype(f32)
            top = jnp.maximum(top, jnp.max(jnp.sum(part * part, axis=1, keepdims=True), axis=0, keepdims=True))
        knorm[0] = jnp.max(top)

    def chosen(blocks, keep):
        found = jnp.zeros(blocks.shape, jnp.bool_)
        for i in range(NSEL):
            found = found | (blocks == sel_ref[tile, i])
        return found & keep

    def chosen_peer(owner):
        found = jnp.zeros(owner.shape, jnp.bool_)
        for i in range(NSEL):
            entry = sel_ref[tile, i]
            found = found | ((owner * per <= entry) & (entry < owner * per + per))
        return found & (owner >= 0)

    def window_parts(shape, dim):
        pos = me * local + tile * TILE - WINDOW + lax.broadcasted_iota(jnp.int32, shape, dim)
        own = chosen(pos // BLK_S, pos >= me * local)
        return pos >= 0, own

    def peer_part(shape, dim):
        slot = lax.broadcasted_iota(jnp.int32, shape, dim) // BLK_S
        return chosen_peer(me - 1 - slot)

    @pl.when(sub == 0)
    def _():
        valid, own = window_parts((1, span), 1)
        valid, own = valid.astype(f32), own.astype(f32)
        begin = pl.multiple_of(tile * TILE, TILE)
        vt = vtw[:, pl.ds(begin, span)].astype(f32)
        lw[:dv] = (vt * valid).astype(bf16)
        lw[dv:2 * dv] = (vt * own).astype(bf16)
        line = lax.broadcasted_iota(jnp.int32, (16, span), 0)
        lw[2 * dv:] = jnp.where(line == 0, valid, jnp.where(line == 1, own, 0.0)).astype(bf16)
        live = peer_part((1, npk), 1).astype(f32)
        lp[:dv] = (vtp[:, :npk].astype(f32) * live).astype(bf16)
        line = lax.broadcasted_iota(jnp.int32, (16, npk), 0)
        lp[dv:] = jnp.where(line == 0, live, 0.0).astype(bf16)

    q = jnp.concatenate([q_ref[h] for h in range(HEADS)], axis=1)

    def gate(c):
        first = c * hc + sub * HEADS
        return jnp.concatenate([g_ref[pl.ds(first + h, 1), :] for h in range(HEADS)], axis=1)

    gate_c, gate_f, gate_w = gate(0), gate(1), gate(2)
    begin = pl.multiple_of(tile * TILE, TILE)
    keys_w = kw[pl.ds(begin, span), :]
    keys_p = bk_ref[:npk, :]
    square = q.astype(f32)
    qn = dot(jnp.ones((8, dk), bf16), (square * square).astype(bf16))
    safe = jnp.max(qn) * knorm[0] * (1.02 * coef * coef) < BOUND * BOUND

    def token(shape):
        return lax.rem(lax.broadcasted_iota(jnp.int32, shape, 1), TILE)

    def coarse_mask():
        shape = (nc, rows)
        end = lax.broadcasted_iota(jnp.int32, shape, 0) * BLK_C + (BLK_C - 1)
        return end <= token(shape) + (me * local + tile * TILE)

    def put(mixed):
        for h in range(HEADS):
            mixed_ref[pl.ds(sub * HEADS + h, TILE, stride=hc), :] = mixed[:, h * TILE:(h + 1) * TILE].T

    @pl.when(safe)
    def _():
        scale = coef * 1.4426950408889634
        ew = jnp.exp2(dot(keys_w, q) * scale)
        key = lax.broadcasted_iota(jnp.int32, (TILE, rows), 0)
        tok = token((TILE, rows))
        low = jnp.where(key > tok, ew[:TILE], 0.0)
        high = jnp.where(key <= tok, ew[WINDOW:], 0.0)
        ew = jnp.concatenate(
            [low.astype(bf16), ew[TILE:WINDOW].astype(bf16), high.astype(bf16)], axis=0
        )
        ow = dot(lw[...], ew)
        ep = jnp.exp2(dot(keys_p, q) * scale).astype(bf16)
        op = dot(lp[...], ep)
        ec = jnp.exp2(dot(ck_ref[...], q) * scale)
        oc = dot(lc[...], jnp.where(coarse_mask(), ec, 0.0).astype(bf16))
        tw = ow[2 * dv:2 * dv + 1]
        tf = ow[2 * dv + 1:2 * dv + 2] + op[dv:dv + 1]
        tc = oc[dv:dv + 1]

        def share(gate, total):
            return jnp.where(total > 0.0, gate / jnp.where(total > 0.0, total, 1.0), 0.0)

        mixed = (
            share(gate_c, tc) * oc[:dv]
            + share(gate_f, tf) * (ow[dv:2 * dv] + op[:dv])
            + share(gate_w, tw) * ow[:dv]
        )
        put(mixed)

    @pl.when(jnp.logical_not(safe))
    def _():
        tok = token((span, rows))
        key = lax.broadcasted_iota(jnp.int32, (span, rows), 0)
        valid, own = window_parts((span, rows), 0)
        causal = key - WINDOW <= tok
        sw = dot(keys_w, q) * coef
        sp = dot(keys_p, q) * coef
        sc = dot(ck_ref[...], q) * coef

        def top(scores, allowed):
            return jnp.max(jnp.where(allowed, scores, -1e30), axis=0, keepdims=True)

        def weigh(scores, allowed, high):
            e = jnp.where(allowed, jnp.exp(jnp.where(allowed, scores - high, 0.0)), 0.0)
            return e.astype(bf16), jnp.sum(e, axis=0, keepdims=True)

        vt = vtw[:, pl.ds(begin, span)]
        ok = valid & causal & (key > tok)
        e, total = weigh(sw, ok, top(sw, ok))
        out_w = dot(vt, e) / jnp.maximum(total, 1.0)
        ok = own & causal
        live = peer_part((npk, rows), 0)
        high = jnp.maximum(top(sw, ok), top(sp, live))
        e, total = weigh(sw, ok, high)
        ep, more = weigh(sp, live, high)
        out_f = (dot(vt, e) + dot(vtp[:, :npk], ep)) / jnp.maximum(total + more, 1.0)
        ok = coarse_mask()
        e, total = weigh(sc, ok, top(sc, ok))
        out_c = dot(lc[:dv], e) / jnp.maximum(total, 1.0)
        mixed = gate_c * out_c + gate_f * out_f + gate_w * out_w
        put(mixed)

    @pl.when(sub == hc // HEADS - 1)
    def _():
        o_ref[...] = mixed_ref[...].astype(bf16)


def on_device(
    n, segs, heads,
    tokens_x, gate_weight, queries, keys, values, comp_key_weight, comp_value_weight, selected,
):
    bf16, f32 = jnp.bfloat16, jnp.float32
    local, hc, dk = queries.shape
    dv = values.shape[2]
    rows_w = gate_weight.shape[0] * gate_weight.shape[1]
    weight = jnp.transpose(gate_weight, (1, 0, 2)).reshape(rows_w, -1)
    share = rows_w // heads
    k2, v2 = keys.reshape(local, dk).T, values.reshape(local, dv)
    chosen = selected.reshape(selected.shape[0], NSEL)
    coarse = local // BLK_C
    vmem = pl.BlockSpec(memory_space=pltpu.VMEM)
    shape = jax.ShapeDtypeStruct
    gates, pk, pv, ck, cv, bk, bv = pl.pallas_call(
        functools.partial(exchange_kernel, n, segs, heads),
        out_shape=[
            shape((share, local), f32),
            shape((dk, local), bf16), shape((local, dv), bf16),
            shape((n * coarse, dk), bf16), shape((n * coarse, dv), bf16),
            shape((n * BLK_S, dk), bf16), shape((n * BLK_S, dv), bf16),
        ],
        in_specs=[vmem] * 7,
        out_specs=[vmem] * 7,
        scratch_shapes=[
            pltpu.VMEM((heads, share, local), f32),
            pltpu.VMEM((heads - 1, share, local), f32),
            pltpu.VMEM((coarse, dk), bf16),
            pltpu.VMEM((coarse, dv), bf16),
            pltpu.VMEM((n - 1,) + chosen.shape, jnp.int32),
            pltpu.VMEM((n - 1, BLK_S, dk), bf16),
            pltpu.VMEM((n - 1, BLK_S, dv), bf16),
            pltpu.SemaphoreType.DMA((6, n)),
            pltpu.SemaphoreType.DMA((6, n)),
            pltpu.SemaphoreType.DMA((heads,)),
            pltpu.SemaphoreType.DMA((heads,)),
        ],
        compiler_params=pltpu.CompilerParams(collective_id=0, has_side_effects=True),
        name="exchange",
    )(tokens_x, weight, k2, v2, comp_key_weight[0], comp_value_weight[0], chosen)

    rows = TILE * hc
    span = WINDOW + TILE
    npk = (n - 1) * BLK_S
    out = pl.pallas_call(
        functools.partial(attention_kernel, n, segs, hc, local),
        grid=(local // TILE, hc // HEADS),
        out_shape=shape((local * hc, dv), bf16),
        in_specs=[
            pl.BlockSpec(memory_space=pltpu.SMEM),
            pl.BlockSpec((HEADS, dk, TILE), lambda i, j: (j, 0, i)),
        ] + [vmem] * 8 + [pl.BlockSpec((share, TILE), lambda i, j: (0, i))],
        out_specs=pl.BlockSpec((rows, dv), lambda i, j: (i, 0)),
        scratch_shapes=[
            pltpu.VMEM((WINDOW + local, dk), bf16),
            pltpu.VMEM((dv, WINDOW + local), bf16),
            pltpu.VMEM((dv, n * BLK_S), bf16),
            pltpu.VMEM((2 * dv + 16, span), bf16),
            pltpu.VMEM((dv + 16, npk), bf16),
            pltpu.VMEM((dv + 16, n * coarse), bf16),
            pltpu.VMEM((rows, dv), f32),
            pltpu.SMEM((1,), f32),
        ],
        compiler_params=pltpu.CompilerParams(
            dimension_semantics=("arbitrary", "arbitrary"), vmem_limit_bytes=60 * 1024 * 1024
        ),
        name="attend",
    )(chosen, jnp.transpose(queries, (1, 2, 0)), k2, v2, pk, pv, bk, bv, ck, cv, gates)
    return out.reshape(local, hc, dv)


def solution(mesh):
    in_specs = (
        P(("ctx", "seg"), "head"),
        P(None, None, "head"),
        P(("ctx", "seg"), "head", None),
        P(("ctx", "seg"), "head", None),
        P(("ctx", "seg"), "head", None),
        P("head", None, None),
        P("head", None, None),
        P(("ctx", "seg"), "head", None),
    )
    n = mesh.shape["ctx"] * mesh.shape["seg"]
    return jax.shard_map(
        functools.partial(on_device, n, mesh.shape["seg"], mesh.shape["head"]),
        mesh=mesh, in_specs=in_specs, out_specs=P(("ctx", "seg"), "head", None), check_vma=False,
    )
```

time: 228 us -> 96.6 us (0.42)
  matrix products: 100 us -> 0 us
  Pallas kernels: 0 us -> 95.9 us
  other arithmetic: 39.5 us -> 0 us
  waiting for transfers between devices: 21.5 us -> 0 us
  local copies, waits for them, and re-layouts: 20.6 us -> 0 us
  blocking collectives: 15.6 us -> 0 us
  between operations: 15 us -> 0.01 us
  loops' own time: 11.2 us -> 0 us
  starting transfers between devices: 2.5 us -> 0 us
    pallas_call x0 -> x2, Pallas kernels: none -> 95.9 us  [the longest x1 73.8 us: on_device(): pl.pallas_call(functools.partial(attention_kernel, n, segs, hc, local), g...]
    dot_general x17 -> x0, matrix products: 65.8 us -> none  [the longest x12 46.3 us: attend(): jnp.einsum('hrk,kv->rhv', rounded, values_part, preferred_element_type=jn...]
    sub x8 -> x0, matrix products: 34.5 us -> none  [attend(): weights = jnp.where(allowed[None], jnp.exp(scores - highest), 0.0)]
    sub x8 -> x0, other arithmetic: 33.2 us -> none  [the longest x4 33.2 us: attend(): weights = jnp.where(allowed[None], jnp.exp(scores - highest), 0.0)]
    all_gather x1 -> x0, blocking collectives: 15.6 us -> none  [on_device(): coarse = lax.all_gather(coarse_packed, ('ctx', 'seg'), axis=0, tiled=True)]
    all_gather x1 -> x0, waiting for transfers between devices: 15.5 us -> none  [on_device(): everything = lax.all_gather(packed, ('ctx', 'seg'), axis=0, tiled=True)]
    another operation x1 -> x0, loops' own time: 11.2 us -> none  [on_device(): tiles = lax.map(one_tile, jnp.arange(local_count // TILE, dtype=jnp.int32))]
    dynamic_slice x8 -> x0, local copies, waits for them, and re-layouts: 7.47 us -> none  [the longest x4 4.88 us: one_tile(): fine = picked[tile].reshape(NSEL * BLK_S, packed.shape[1])]
  transfers between devices with their start and end apart: 3 -> 0, of which waited for: 2 -> 0; matrix products, arithmetic and copies ran while one was open for 2% -> 0% of each run, Pallas kernels for 0% -> 0%
where the time goes in v1:
time: 96.6 us; the launch traced here: 95.9 us
  Pallas kernels  95.9 us (99%)
    pallas_call x1, Pallas kernels, on_device(): pl.pallas_call(functools.partial(attention_kernel, n, segs, hc, local), g...  73.8 us
    pallas_call x1, Pallas kernels, on_device(): pl.pallas_call(functools.partial(exchange_kernel, n, segs, heads), out_sh...  22 us

profile of v1, /device:TPU:0, one launch (start us, length us, event | category | flops | bytes accessed | tf_op | source)
XLA Modules:
  0.0 95.9 jit_solution(11092575796532296801)
XLA Ops:
  0.0 22.0 %exchange.1 = (f32[48,512]{1,0:T(8,128)}, bf16[192,512]{1,0:T(8,128)(2,1)}, bf16[512,128]{1,0:T(8,128)(2,1)}, bf16[128,192]{1,0:T(8,128)(2,1)}, bf16[128,128]{1,...) custom-call(bf16[512,640]{1,0:T(8,128)(2,1)} %x_ref.1, bf16[192,640]{1,0:T(8,128)(2,1)} %bitcast.17, ...), custom_call_target="tpu_custom_call" | custom-call | tf_op jit(solution)/shard_map/exchange/pallas_call | solution.py:309
  22.0 73.8 %attend.1 = bf16[8192,128]{1,0:T(8,128)(2,1)} custom-call(s32[4,16]{1,0:T(4,128)} %bitcast.21, bf16[16,192,512]{2,1,0:T(8,128)(2,1)} %bitcast.12, bf16[192,512]{1,0:T(8,128)(2,1)} %bitcast.14, bf16[512,128]{1,0:T(8,128)(2,1)} %bitcast.16, bf16[192,512]{1,0:T(8,128)(2,1)} %get-tuple-element.12.pk_ref, bf16[512,128]{1,0:T(8,128)(2,1)} %get-tuple-element.13.pv_ref, ...), custom_call_target="tpu_custom_call" | custom-call | tf_op jit(solution)/shard_map/attend/pallas_call | solution.py:339

commit v2 on v1

--- a/solution.py
+++ b/solution.py
@@ -12,7 +12,7 @@
 BLK_C = 32
 NSEL = 16
 WINDOW = 512
-HEADS = 4
+KEY_ROWS = 1 << 22
 BOUND = 40.0
 
 MESH = pl.DeviceIdType.MESH
@@ -26,9 +26,9 @@
 
 def exchange_kernel(
     n, segs, heads,
-    x_ref, w_ref, kt_ref, v_ref, cwk_ref, cwv_ref, sel_ref,
-    g_ref, pk_ref, pv_ref, ck_ref, cv_ref, bk_ref, bv_ref,
-    part, got, cks, cvs, sels, stk, stv, ssem, rsem, gs, gr,
+    x_ref, w_ref, kt_ref, v_ref, cwk_ref, cwv_ref, sel_ref, q_hbm,
+    g_ref, pk_ref, pv_ref, ck_ref, cv_ref, bk_ref, bv_ref, qn_ref,
+    part, got, cks, cvs, sels, stk, stv, qs, ssem, rsem, gs, gr, qsem,
 ):
     local = v_ref.shape[0]
     coarse = local // BLK_C
@@ -43,6 +43,8 @@
     def peer(steps):
         return {"head": lax.rem(head + steps + heads, heads)}
 
+    fetch = pltpu.make_async_copy(q_hbm, qs, qsem)
+    fetch.start()
     barrier = pltpu.get_barrier_semaphore()
     for r in range(1, n):
         pl.semaphore_signal(barrier, inc=1, device_id=ring(r), device_id_type=MESH)
@@ -114,6 +116,15 @@
         rest.append(send(stk.at[r - 1], bk_ref.at[rows], 3, r - 1, ring(r)))
         rest.append(send(stv.at[r - 1], bv_ref.at[rows], 4, r - 1, ring(r)))
 
+    fetch.wait()
+
+    def norm(h, best):
+        q = qs[h].astype(jnp.float32)
+        return jnp.maximum(best, jnp.sum(q * q, axis=0, keepdims=True))
+
+    best = lax.fori_loop(0, qs.shape[0], norm, jnp.zeros((1, local), jnp.float32))
+    qn_ref[...] = jnp.broadcast_to(best, qn_ref.shape)
+
     for copy in sums:
         copy.wait()
     total = part[head]
@@ -125,16 +136,16 @@
 
 
 def attention_kernel(
-    n, segs, hc, local,
-    sel_ref, q_ref, kt_ref, v_ref, pk_ref, pv_ref, bk_ref, bv_ref, ck_ref, cv_ref, g_ref,
+    n, segs, hc, local, step_heads,
+    sel_ref, q_ref, kt_ref, v_ref, pk_ref, pv_ref, bk_ref, bv_ref, ck_ref, cv_ref, qn_ref, g_ref,
     o_ref,
-    kw, vtw, vtp, lw, lp, lc, mixed_ref, knorm,
+    kw, vtw, vtp, lw, lp, lc, mixed_ref, flag,
 ):
     f32, bf16 = jnp.float32, jnp.bfloat16
     me = lax.axis_index("ctx") * segs + lax.axis_index("seg")
     tile = pl.program_id(0)
     sub = pl.program_id(1)
-    rows = TILE * HEADS
+    rows = TILE * step_heads
     span = WINDOW + TILE
     dk = kt_ref.shape[0]
     dv = v_ref.shape[1]
@@ -158,7 +169,8 @@
         for ref in (kw, bk_ref, ck_ref):
             part = ref[...].astype(f32)
             top = jnp.maximum(top, jnp.max(jnp.sum(part * part, axis=1, keepdims=True), axis=0, keepdims=True))
-        knorm[0] = jnp.max(top)
+        worst = jnp.max(qn_ref[...]) * jnp.max(top) * (1.02 * coef * coef)
+        flag[0] = jnp.where(worst < BOUND * BOUND, 1, 0)
 
     def chosen(blocks, keep):
         found = jnp.zeros(blocks.shape, jnp.bool_)
@@ -197,19 +209,17 @@
         line = lax.broadcasted_iota(jnp.int32, (16, npk), 0)
         lp[dv:] = jnp.where(line == 0, live, 0.0).astype(bf16)
 
-    q = jnp.concatenate([q_ref[h] for h in range(HEADS)], axis=1)
+    q = jnp.concatenate([q_ref[h] for h in range(step_heads)], axis=1)
 
     def gate(c):
-        first = c * hc + sub * HEADS
-        return jnp.concatenate([g_ref[pl.ds(first + h, 1), :] for h in range(HEADS)], axis=1)
+        first = c * hc + sub * step_heads
+        return jnp.concatenate([g_ref[pl.ds(first + h, 1), :] for h in range(step_heads)], axis=1)
 
     gate_c, gate_f, gate_w = gate(0), gate(1), gate(2)
     begin = pl.multiple_of(tile * TILE, TILE)
     keys_w = kw[pl.ds(begin, span), :]
     keys_p = bk_ref[:npk, :]
-    square = q.astype(f32)
-    qn = dot(jnp.ones((8, dk), bf16), (square * square).astype(bf16))
-    safe = jnp.max(qn) * knorm[0] * (1.02 * coef * coef) < BOUND * BOUND
+    safe = flag[0] == 1
 
     def token(shape):
         return lax.rem(lax.broadcasted_iota(jnp.int32, shape, 1), TILE)
@@ -220,8 +230,8 @@
         return end <= token(shape) + (me * local + tile * TILE)
 
     def put(mixed):
-        for h in range(HEADS):
-            mixed_ref[pl.ds(sub * HEADS + h, TILE, stride=hc), :] = mixed[:, h * TILE:(h + 1) * TILE].T
+        for h in range(step_heads):
+            mixed_ref[pl.ds(sub * step_heads + h, TILE, stride=hc), :] = mixed[:, h * TILE:(h + 1) * TILE].T
 
     @pl.when(safe)
     def _():
@@ -286,7 +296,7 @@
         mixed = gate_c * out_c + gate_f * out_f + gate_w * out_w
         put(mixed)
 
-    @pl.when(sub == hc // HEADS - 1)
+    @pl.when(sub == hc // step_heads - 1)
     def _():
         o_ref[...] = mixed_ref[...].astype(bf16)
 
@@ -306,16 +316,18 @@
     coarse = local // BLK_C
     vmem = pl.BlockSpec(memory_space=pltpu.VMEM)
     shape = jax.ShapeDtypeStruct
-    gates, pk, pv, ck, cv, bk, bv = pl.pallas_call(
+    q3 = jnp.transpose(queries, (1, 2, 0))
+    gates, pk, pv, ck, cv, bk, bv, qn = pl.pallas_call(
         functools.partial(exchange_kernel, n, segs, heads),
         out_shape=[
             shape((share, local), f32),
             shape((dk, local), bf16), shape((local, dv), bf16),
             shape((n * coarse, dk), bf16), shape((n * coarse, dv), bf16),
             shape((n * BLK_S, dk), bf16), shape((n * BLK_S, dv), bf16),
+            shape((8, local), f32),
         ],
-        in_specs=[vmem] * 7,
-        out_specs=[vmem] * 7,
+        in_specs=[vmem] * 7 + [pl.BlockSpec(memory_space=pl.ANY)],
+        out_specs=[vmem] * 8,
         scratch_shapes=[
             pltpu.VMEM((heads, share, local), f32),
             pltpu.VMEM((heads - 1, share, local), f32),
@@ -324,26 +336,32 @@
             pltpu.VMEM((n - 1,) + chosen.shape, jnp.int32),
             pltpu.VMEM((n - 1, BLK_S, dk), bf16),
             pltpu.VMEM((n - 1, BLK_S, dv), bf16),
+            pltpu.VMEM((hc, dk, local), bf16),
             pltpu.SemaphoreType.DMA((6, n)),
             pltpu.SemaphoreType.DMA((6, n)),
             pltpu.SemaphoreType.DMA((heads,)),
             pltpu.SemaphoreType.DMA((heads,)),
+            pltpu.SemaphoreType.DMA,
         ],
         compiler_params=pltpu.CompilerParams(collective_id=0, has_side_effects=True),
         name="exchange",
-    )(tokens_x, weight, k2, v2, comp_key_weight[0], comp_value_weight[0], chosen)
+    )(tokens_x, weight, k2, v2, comp_key_weight[0], comp_value_weight[0], chosen, q3)
 
     rows = TILE * hc
     span = WINDOW + TILE
     npk = (n - 1) * BLK_S
+    width = span + npk + n * coarse
+    step_heads = hc
+    while step_heads > 2 and step_heads * TILE * width > KEY_ROWS:
+        step_heads //= 2
     out = pl.pallas_call(
-        functools.partial(attention_kernel, n, segs, hc, local),
-        grid=(local // TILE, hc // HEADS),
+        functools.partial(attention_kernel, n, segs, hc, local, step_heads),
+        grid=(local // TILE, hc // step_heads),
         out_shape=shape((local * hc, dv), bf16),
         in_specs=[
             pl.BlockSpec(memory_space=pltpu.SMEM),
-            pl.BlockSpec((HEADS, dk, TILE), lambda i, j: (j, 0, i)),
-        ] + [vmem] * 8 + [pl.BlockSpec((share, TILE), lambda i, j: (0, i))],
+            pl.BlockSpec((step_heads, dk, TILE), lambda i, j: (j, 0, i)),
+        ] + [vmem] * 9 + [pl.BlockSpec((share, TILE), lambda i, j: (0, i))],
         out_specs=pl.BlockSpec((rows, dv), lambda i, j: (i, 0)),
         scratch_shapes=[
             pltpu.VMEM((WINDOW + local, dk), bf16),
@@ -353,13 +371,13 @@
             pltpu.VMEM((dv + 16, npk), bf16),
             pltpu.VMEM((dv + 16, n * coarse), bf16),
             pltpu.VMEM((rows, dv), f32),
-            pltpu.SMEM((1,), f32),
+            pltpu.SMEM((1,), jnp.int32),
         ],
         compiler_params=pltpu.CompilerParams(
             dimension_semantics=("arbitrary", "arbitrary"), vmem_limit_bytes=60 * 1024 * 1024
         ),
         name="attend",
-    )(chosen, jnp.transpose(queries, (1, 2, 0)), k2, v2, pk, pv, bk, bv, ck, cv, gates)
+    )(chosen, q3, k2, v2, pk, pv, bk, bv, ck, cv, qn, gates)
     return out.reshape(local, hc, dv)
 
 

time: 96.6 us -> 69.6 us (0.72)
  Pallas kernels: 95.9 us -> 68.8 us
    pallas_call x1, Pallas kernels: 73.8 us -> 46.8 us  [on_device(): pl.pallas_call(functools.partial(attention_kernel, n, segs, hc, local, st...]
where the time goes in v2:
time: 69.6 us; the launch traced here: 68.8 us
  Pallas kernels  68.8 us (99%)
    pallas_call x1, Pallas kernels, on_device(): pl.pallas_call(functools.partial(attention_kernel, n, segs, hc, local, st...  46.8 us
    pallas_call x1, Pallas kernels, on_device(): pl.pallas_call(functools.partial(exchange_kernel, n, segs, heads), out_sh...  22 us

profile of v2, /device:TPU:0, one launch (start us, length us, event | category | flops | bytes accessed | tf_op | source)
XLA Modules:
  0.0 68.8 jit_solution(11314956922857639603)
XLA Ops:
  0.0 22.0 %exchange.1 = (f32[48,512]{1,0:T(8,128)}, bf16[192,512]{1,0:T(8,128)(2,1)}, bf16[512,128]{1,0:T(8,128)(2,1)}, bf16[128,192]{1,0:T(8,128)(2,1)}, bf16[128,128]{1,...) custom-call(bf16[512,640]{1,0:T(8,128)(2,1)} %x_ref.1, ...), custom_call_target="tpu_custom_call" | custom-call | tf_op jit(solution)/shard_map/exchange/pallas_call | solution.py:320
  22.1 46.8 %attend.1 = bf16[8192,128]{1,0:T(8,128)(2,1)} custom-call(s32[4,16]{1,0:T(4,128)} %bitcast.22, bf16[16,192,512]{2,1,0:T(8,128)(2,1)} %bitcast.13, bf16[192,512]{1,0:T(8,128)(2,1)} %bitcast.15, bf16[512,128]{1,0:T(8,128)(2,1)} %bitcast.17, bf16[192,512]{1,0:T(8,128)(2,1)} %get-tuple-element.13.pk_ref, bf16[512,128]{1,0:T(8,128)(2,1)} %get-tuple-element.14.pv_ref, ...), custom_call_target="tpu_custom_call" | custom-call | tf_op jit(solution)/shard_map/attend/pallas_call | solution.py:357
